TPU v7x, 32 devices: a whole 2x2x4 slice. The times are simulated.
32 devices in a mesh: gx: 4 (over y, core), gy: 8 (over z, x).
Axes of the slice: x: 2, y: 2, z: 4, core: 2. Of those that a mesh axis runs over, the one named last changes fastest.
Arguments:
- perturbation: float32 [5, 16, 512], P(None, 'gx', 'gy'), may hold values from -6 to 6
- mean_velocity: float32 [16, 512], P('gx', 'gy'), may hold values from 0.2 to 0.9
- mean_shear: float32 [16, 512], P('gx', 'gy'), may hold values from -4 to 4
- cotangent: float32 [5, 16, 512], P(None, 'gx', 'gy'), may hold values from -6 to 6
- kernel_in: bfloat16 [64, 135], replicated, may hold values from -0.5 to 0.5
- kernel_mid: bfloat16 [64, 1728], replicated, may hold values from -0.15625 to 0.15625
- kernel_out: bfloat16 [5, 1728], replicated, may hold values from -0.15625 to 0.15625
Outputs:
- advanced: float32 [5, 16, 512], P(None, 'gx', 'gy')
- grad_in: float32 [64, 135], replicated
- grad_mid: float32 [64, 1728], replicated
- grad_out: float32 [5, 1728], replicated
All inputs are finite; a program needn't handle non-finite values.
Results may differ from a plain program's by a relative error of at most 0.0065.
Values may be sent and summed in bfloat16 or wider, within the bound.
A program may use at most 64 MiB of HBM per device.

v0:
```python
import math
import jax
import jax.numpy as jnp
from jax import lax
from jax.sharding import PartitionSpec as P

NZ = 8
STEPS = 2
TIME_STEP = 0.25
STENCIL_WEIGHTS = (0.75, -0.15, 1.0 / 60.0)


def padded_2(cells, sides, width):
    for axis, dim in sides:
        count = lax.axis_size(axis)
        ends = count - 1
        head = lax.slice_in_dim(cells, 0, width, axis=dim)
        tail = lax.slice_in_dim(cells, cells.shape[dim] - width, cells.shape[dim], axis=dim)
        cells = jnp.concatenate(
            [
                lax.ppermute(tail, axis, [(i, (i + 1) % count) for i in range(ends)]),
                cells,
                lax.ppermute(head, axis, [((i + 1) % count, i) for i in range(ends)]),
            ],
            axis=dim,
        )
    return cells


def wrap_depth(grid_field, margin):
    size_z = grid_field.shape[3]
    return jnp.concatenate(
        [grid_field[:, :, :, size_z - margin :], grid_field, grid_field[:, :, :, :margin]], axis=3
    )


def difference(padded, direction, margin, length):
    summed = None
    for offset, weight in zip((1, 2, 3), STENCIL_WEIGHTS):
        upper_cells = lax.slice_in_dim(
            padded, margin + offset, margin + offset + length, axis=direction
        )
        lower_cells = lax.slice_in_dim(
            padded, margin - offset, margin - offset + length, axis=direction
        )
        contrib = weight * (upper_cells - lower_cells)
        summed = contrib if summed is None else summed + contrib
    return summed


def rates_from(padded, margin, velocity, shear_rate):
    size_x = padded.shape[1] - 2 * margin
    size_y = padded.shape[2] - 2 * margin
    interior = padded[:, margin : margin + size_x, margin : margin + size_y]
    slope_x = difference(padded[:, :, margin : margin + size_y], 1, margin, size_x)
    slope_y = difference(padded[:, margin : margin + size_x], 2, margin, size_y)
    slope_z = difference(wrap_depth(interior, 3), 3, 3, interior.shape[3])
    divergence = slope_x[1] + slope_y[2] + slope_z[3]
    return jnp.stack(
        [
            -velocity * slope_x[0] - divergence,
            -velocity * slope_x[1] - shear_rate * interior[2] - slope_x[4],
            -velocity * slope_x[2] - slope_y[4],
            -velocity * slope_x[3] - slope_z[4],
            -velocity * slope_x[4] - divergence,
        ]
    )


def adjoint_fields(adjoint_in, velocity):
    acoustic = adjoint_in[0] + adjoint_in[4]
    return jnp.stack(
        [
            velocity * adjoint_in[0],
            velocity * adjoint_in[1] + acoustic,
            velocity * adjoint_in[2],
            velocity * adjoint_in[3],
            velocity * adjoint_in[4] + adjoint_in[1],
            acoustic,
            adjoint_in[2],
            adjoint_in[3],
        ]
    )


def adjoint_from(padded, margin, adjoint_in, shear_rate):
    size_x = padded.shape[1] - 2 * margin
    size_y = padded.shape[2] - 2 * margin
    interior = padded[:, margin : margin + size_x, margin : margin + size_y]
    slope_x = difference(padded[:5, :, margin : margin + size_y], 1, margin, size_x)
    slope_y = difference(padded[5:, margin : margin + size_x], 2, margin, size_y)
    slope_z = difference(wrap_depth(interior[5:], 3), 3, 3, interior.shape[3])
    return jnp.stack(
        [
            slope_x[0],
            slope_x[1],
            slope_x[2] - shear_rate * adjoint_in[1] + slope_y[0],
            slope_x[3] + slope_z[0],
            slope_x[4] + slope_y[1] + slope_z[2],
        ]
    )


def conv_valid(padded, kernel):
    return lax.conv_general_dilated(
        padded[None],
        kernel,
        (1, 1, 1),
        "VALID",
        dimension_numbers=("NCDHW", "OIDHW", "NCDHW"),
        preferred_element_type=jnp.float32,
    )[0]


def flip_kernel(kernel):
    return jnp.transpose(jnp.flip(kernel, (2, 3, 4)), (1, 0, 2, 3, 4))


def kernel_grad(padded, gradient):
    channels = padded.shape[0]
    size_x, size_y, size_z = (gradient.shape[1], gradient.shape[2], gradient.shape[3])
    flat_grad = gradient.reshape(gradient.shape[0], -1)
    pieces = []
    for shift_x in range(3):
        for shift_y in range(3):
            for shift_z in range(3):
                window = padded[
                    :,
                    shift_x : shift_x + size_x,
                    shift_y : shift_y + size_y,
                    shift_z : shift_z + size_z,
                ]
                pieces.append(
                    lax.dot_general(
                        flat_grad,
                        window.reshape(channels, -1),
                        (((1,), (1,)), ((), ())),
                        preferred_element_type=jnp.float32,
                    )
                )
    stacked = jnp.stack(pieces)
    return jnp.transpose(stacked, (1, 2, 0)).reshape(gradient.shape[0], channels * 27)


def closure_backward(saved, source_grad, kernels, need_input, padding_fn):
    kernel_in, kernel_mid, kernel_out = kernels
    padded_in, hidden_one, padded_one, hidden_two, padded_two = saved
    error_out = source_grad.astype(jnp.bfloat16)
    grad_out = kernel_grad(padded_two, error_out)
    back_mid = conv_valid(padding_fn(error_out), flip_kernel(kernel_out)) * (
        1.0 - jnp.square(hidden_two.astype(jnp.float32))
    )
    error_mid = back_mid.astype(jnp.bfloat16)
    grad_mid = kernel_grad(padded_one, error_mid)
    back_in = conv_valid(padding_fn(error_mid), flip_kernel(kernel_mid)) * (
        1.0 - jnp.square(hidden_one.astype(jnp.float32))
    )
    error_in = back_in.astype(jnp.bfloat16)
    grad_in = kernel_grad(padded_in, error_in)
    state_grad = conv_valid(padding_fn(error_in), flip_kernel(kernel_in)) if need_input else None
    return ((grad_in, grad_mid, grad_out), state_grad)


def retreat(adjoint_in, adjoint_fn):
    into_second = 2.0 / 3.0 * adjoint_in + 2.0 / 3.0 * TIME_STEP * adjoint_fn(adjoint_in)
    direct = 1.0 / 3.0 * adjoint_in
    into_first = 0.25 * into_second + 0.25 * TIME_STEP * adjoint_fn(into_second)
    direct = direct + 0.75 * into_second
    carried = direct + into_first + TIME_STEP * adjoint_fn(into_first)
    source_grad = TIME_STEP * (2.0 / 3.0 * adjoint_in + 0.25 * into_second + into_first)
    return (carried, source_grad)


def grad_pad(grid_field):
    return wrap_depth(padded_2(grid_field, (("gx", 1), ("gy", 2)), 1), 1)


def inside(size_x, size_y, margin):
    start_x = lax.axis_index("gx") * size_x - margin
    start_y = lax.axis_index("gy") * size_y - margin
    index_x = start_x + jnp.arange(size_x + 2 * margin, dtype=jnp.int32)
    index_y = start_y + jnp.arange(size_y + 2 * margin, dtype=jnp.int32)
    valid_x = (index_x >= 0) & (index_x < size_x * lax.axis_size("gx"))
    valid_y = (index_y >= 0) & (index_y < size_y * lax.axis_size("gy"))
    return (valid_x[:, None] & valid_y[None, :]).astype(jnp.float32)[None, :, :, None]


def closure_deep(grid_field, kernels):
    kernel_in, kernel_mid, kernel_out = kernels
    size_x, size_y = (grid_field.shape[1], grid_field.shape[2])
    extended = padded_2(grid_field, (("gx", 1), ("gy", 2)), 3)
    input_wide = extended.astype(jnp.bfloat16)
    hidden_wide = (
        jnp.tanh(conv_valid(wrap_depth(input_wide, 1), kernel_in)) * inside(size_x, size_y, 2)
    ).astype(jnp.bfloat16)
    second_wide = (
        jnp.tanh(conv_valid(wrap_depth(hidden_wide, 1), kernel_mid)) * inside(size_x, size_y, 1)
    ).astype(jnp.bfloat16)
    source = conv_valid(wrap_depth(second_wide, 1), kernel_out)
    saved = (
        wrap_depth(input_wide[:, 2:-2, 2:-2], 1),
        hidden_wide[:, 2:-2, 2:-2],
        wrap_depth(hidden_wide[:, 1:-1, 1:-1], 1),
        second_wide[:, 1:-1, 1:-1],
        wrap_depth(second_wide, 1),
    )
    return (extended, source, saved)


def body(perturbation, mean_velocity, mean_shear, cotangent, kernel_in, kernel_mid, kernel_out):
    channels = perturbation.shape[0]
    hidden = kernel_in.shape[0]
    size_x = perturbation.shape[1]
    size_y = perturbation.shape[2] // NZ
    current = perturbation.reshape(channels, size_x, size_y, NZ)
    velocity = mean_velocity.reshape(size_x, size_y, NZ)
    shear_rate = mean_shear.reshape(size_x, size_y, NZ)
    kernels = (
        kernel_in.reshape(hidden, channels, 3, 3, 3),
        kernel_mid.reshape(hidden, hidden, 3, 3, 3),
        kernel_out.reshape(channels, hidden, 3, 3, 3),
    )

    def section_rates(grid_field):
        padded = padded_2(grid_field, (("gx", 1), ("gy", 2)), 3)
        return rates_from(padded, 3, velocity, shear_rate)

    def adjoint_rates(adjoint_in):
        padded = padded_2(adjoint_fields(adjoint_in, velocity), (("gx", 1), ("gy", 2)), 3)
        return adjoint_from(padded, 3, adjoint_in, shear_rate)

    def evaluate(grid_field, with_rates):
        extended, source, saved = closure_deep(grid_field, kernels)
        rate_field = rates_from(extended, 3, velocity, shear_rate) if with_rates else None
        return (source, saved, rate_field)

    history = []
    stored = []
    for step_index in range(STEPS):
        source, saved, rate_field = evaluate(current, True)
        history.append(current)
        stored.append(saved)
        section_one = current + TIME_STEP * (rate_field + source)
        section_two = 0.75 * current + 0.25 * (
            section_one + TIME_STEP * (section_rates(section_one) + source)
        )
        current = 1.0 / 3.0 * current + 2.0 / 3.0 * (
            section_two + TIME_STEP * (section_rates(section_two) + source)
        )
    cell_count = size_x * lax.axis_size("gx") * size_y * lax.axis_size("gy") * NZ
    adjoint_in = cotangent.reshape(channels, size_x, size_y, NZ) * (1.0 / math.sqrt(cell_count))
    totals = None
    for step_index in reversed(range(STEPS)):
        carried, source_grad = retreat(adjoint_in, adjoint_rates)
        saved = evaluate(history[step_index], False)[1]
        kernel_grads, state_grad = closure_backward(
            saved, source_grad, kernels, step_index > 0, grad_pad
        )
        totals = (
            kernel_grads
            if totals is None
            else tuple((sum_old + sum_new for sum_old, sum_new in zip(totals, kernel_grads)))
        )
        if step_index > 0:
            adjoint_in = carried + state_grad
    result = lax.psum((totals[0], totals[1], totals[2]), ("gx", "gy"))
    return (current.reshape(channels, size_x, size_y * NZ), result[0], result[1], result[2])


def solution(mesh):
    return jax.shard_map(
        body,
        mesh=mesh,
        in_specs=(
            P(None, "gx", "gy"),
            P("gx", "gy"),
            P("gx", "gy"),
            P(None, "gx", "gy"),
            P(),
            P(),
            P(),
        ),
        out_specs=(P(None, "gx", "gy"), P(), P(), P()),
        check_vma=False,
    )
```

profile of v0, /device:TPU:0, one launch (start us, length us, event | category | flops | bytes accessed | tf_op | source)
XLA Modules:
  0.0 642.7 jit_solution(11449475301091532205)
XLA Ops:
  8.0 2.4 collective-permute-start.1
  14.4 5.8 collective-permute-start.25
  30.3 3.4 collective-permute-start.3
  35.9 5.2 collective-permute-start.27
  46.2 2.5 convolution_tanh_fusion
  50.0 5.2 fusion.164
  58.3 2.8 fusion.175
  65.7 3.4 collective-permute-start.29
  70.2 4.3 collective-permute-start.31
  77.6 5.0 collective-permute-done.30
  85.2 3.2 collective-permute-start.5
  92.4 7.0 %collective-permute-start.32 = (bf16[5,1,8,8]{3,2,1,0:T(8,128)(2,1)S(1)}, bf16[5,1,8,8]{3,2,1,0:T(8,128)(2,1)S(1)}, u32[]{:S(2)}, u32[]{:S(2)}) collective-permute-start(bf16[5,1,8,8]{3,2,1,0:T(8,128)(2,1)S(1)} %get-tuple-element.302), channel_id=1, source_target_pairs={{0,8},{8,16},{16,24},{1,9},{9,17},{17,25},{2,10},{10,18},{18,26},{... | collective-permute-start | bytes 1928 | tf_op jit(solution)/shard_map/ppermute | solution.py:21
  101.6 5.4 collective-permute-start.34
  107.7 3.3 collective-permute-start.41
  113.8 4.5 collective-permute-start.7
  120.1 4.6 collective-permute-start.43
  126.4 3.9 collective-permute-start.9
  133.9 5.4 collective-permute-start.11
  141.6 5.2 collective-permute-done.10
  147.8 3.7 collective-permute-start.13
  155.3 4.8 collective-permute-start.15
  162.4 4.3 collective-permute-done.14
  170.8 2.5 fusion.691
  174.6 5.2 fusion.162
  181.3 4.2 collective-permute-start.36
  186.6 2.8 fusion.173
  206.7 4.5 collective-permute-start.38
  215.4 3.7 collective-permute-start.44
  232.7 5.0 collective-permute-start.46
  239.0 2.8 fusion.171
  244.2 3.7 collective-permute-start.49
  249.0 4.5 collective-permute-start.51
  256.6 5.3 collective-permute-done.50
  265.2 3.6 collective-permute-start.53
  269.0 5.0 collective-permute-start.17
  277.2 4.8 collective-permute-start.19
  283.7 5.2 collective-permute-start.55
  291.5 5.4 collective-permute-done.54
  299.9 2.8 collective-permute-start.21
  305.6 4.4 collective-permute-start.56
  319.4 4.5 collective-permute-start.58
  329.5 3.5 collective-permute-start.60
  340.2 4.7 collective-permute-start.62
  371.5 4.9 collective-permute-start.23
  379.7 5.2 collective-permute-done.22
  386.8 111.3 %all-reduce.6.cloned.1.call-done = (f32[64,135]{0,1:T(8,128)}, f32[5,1728]{1,0:T(8,128)}) async-done(((f32[64,135]{0,1:T(8,128)}, f32[5,1728]{1,0:T(8,128)}), (f32[64,135]{0,1:T(8,128)}, f32[5,1728]{1,0:T(8,128)})) %all-reduce.6.cloned.1.call-update) | async-done | bytes 69136 | tf_op jit(solution)/shard_map/psum | solution.py:266
  499.7 133.0 %all-reduce.4.cloned.1.call-done = f32[64,1728]{0,1:T(8,128)} async-done(((f32[64,1728]{0,1:T(8,128)}), f32[64,1728]{0,1:T(8,128)}) %all-reduce.4.cloned.1.call-update) | async-done | bytes 442384 | tf_op jit(solution)/shard_map/psum | solution.py:266
  632.7 2.2 copy.1541
  (799 shorter events, 184.5 us)
Async XLA Ops:
  7.2 491.0 %all-reduce.6.cloned.1.call-start = ((), (), s32[]{:S(2)}) async-start(), calls=%async_computation.1 | async-start | bytes 253952 | tf_op jit(solution)/shard_map/psum | solution.py:266
  8.0 21.2 %collective-permute-start.1 = (f32[5,3,8,8]{3,2,1,0:T(8,128)S(1)}, f32[5,3,8,8]{3,2,1,0:T(8,128)S(1)}, u32[]{:S(2)}, u32[]{:S(2)}) collective-permute-start(f32[5,3,8,8]{3,2,1,0:T(8,128)S(1)} %get-tuple-element.273), channel_id=1, source_target_pairs={{0,8},{8,16},{16,24},{1,9},{9,17},{17,25},{2,10},{10,18},{18,26},{... | collective-permute-start | bytes 11528 | tf_op jit(solution)/shard_map/ppermute | solution.py:21
  10.5 19.8 %collective-permute-start = (f32[5,3,8,8]{3,2,1,0:T(8,128)S(1)}, f32[5,3,8,8]{3,2,1,0:T(8,128)S(1)}, u32[]{:S(2)}, u32[]{:S(2)}) collective-permute-start(f32[5,3,8,8]{3,2,1,0:T(8,128)S(1)} %get-tuple-element.272), channel_id=1, source_target_pairs={{8,0},{16,8},{24,16},{9,1},{17,9},{25,17},{10,2},{18,10},{26,18},{... | collective-permute-start | bytes 11528 | tf_op jit(solution)/shard_map/ppermute | solution.py:23
  13.1 21.9 %collective-permute-start.24 = (f32[8,3,8,8]{3,2,1,0:T(8,128)S(1)}, f32[8,3,8,8]{3,2,1,0:T(8,128)S(1)}, u32[]{:S(2)}, u32[]{:S(2)}) collective-permute-start(f32[8,3,8,8]{3,2,1,0:T(8,128)S(1)} %get-tuple-element.202), channel_id=1, source_target_pairs={{8,0},{16,8},{24,16},{9,1},{17,9},{25,17},{10,2},{18,10},{26,18},{... | collective-permute-start | bytes 18440 | tf_op jit(solution)/shard_map/ppermute | solution.py:23
  14.4 20.6 %collective-permute-start.25 = (f32[8,3,8,8]{3,2,1,0:T(8,128)S(1)}, f32[8,3,8,8]{3,2,1,0:T(8,128)S(1)}, u32[]{:S(2)}, u32[]{:S(2)}) collective-permute-start(f32[8,3,8,8]{3,2,1,0:T(8,128)S(1)} %get-tuple-element.201), channel_id=1, source_target_pairs={{0,8},{8,16},{16,24},{1,9},{9,17},{17,25},{2,10},{10,18},{18,26},{... | collective-permute-start | bytes 18440 | tf_op jit(solution)/shard_map/ppermute | solution.py:21
  30.3 12.2 %collective-permute-start.3 = (f32[5,10,3,8]{3,2,1,0:T(4,128)S(1)}, f32[5,10,3,8]{3,2,1,0:T(4,128)S(1)}, u32[]{:S(2)}, u32[]{:S(2)}) collective-permute-start(f32[5,10,3,8]{3,2,1,0:T(4,128)S(1)} %get-tuple-element.153), channel_id=1, source_target_pairs={{0,1},{1,2},{2,3},{3,4},{4,5},{5,6},{6,7},{8,9},{9,10},{10,11},{11... | collective-permute-start | bytes 14408 | tf_op jit(solution)/shard_map/ppermute | solution.py:21
  33.7 8.7 %collective-permute-start.2 = (f32[5,10,3,8]{3,2,1,0:T(4,128)S(1)}, f32[5,10,3,8]{3,2,1,0:T(4,128)S(1)}, u32[]{:S(2)}, u32[]{:S(2)}) collective-permute-start(f32[5,10,3,8]{3,2,1,0:T(4,128)S(1)} %get-tuple-element.152), channel_id=1, source_target_pairs={{1,0},{2,1},{3,2},{4,3},{5,4},{6,5},{7,6},{9,8},{10,9},{11,10},{12... | collective-permute-start | bytes 14408 | tf_op jit(solution)/shard_map/ppermute | solution.py:23
  35.9 27.0 %collective-permute-start.27 = (f32[8,10,3,8]{3,2,1,0:T(4,128)}, f32[8,10,3,8]{3,2,1,0:T(4,128)}, u32[]{:S(2)}, u32[]{:S(2)}) collective-permute-start(f32[8,10,3,8]{3,2,1,0:T(4,128)} %get-tuple-element.95), channel_id=1, source_target_pairs={{0,1},{1,2},{2,3},{3,4},{4,5},{5,6},{6,7},{8,9},{9,10},{10,11},{11... | collective-permute-start | bytes 23048 | tf_op jit(solution)/shard_map/ppermute | solution.py:21
  41.1 21.8 %collective-permute-start.26 = (f32[8,10,3,8]{3,2,1,0:T(4,128)}, f32[8,10,3,8]{3,2,1,0:T(4,128)}, u32[]{:S(2)}, u32[]{:S(2)}) collective-permute-start(f32[8,10,3,8]{3,2,1,0:T(4,128)} %get-tuple-element.94), channel_id=1, source_target_pairs={{1,0},{2,1},{3,2},{4,3},{5,4},{6,5},{7,6},{9,8},{10,9},{11,10},{12... | collective-permute-start | bytes 23048 | tf_op jit(solution)/shard_map/ppermute | solution.py:23
  70.2 7.4 %collective-permute-start.31 = (f32[8,10,3,8]{3,2,1,0:T(4,128)S(1)}, f32[8,10,3,8]{3,2,1,0:T(4,128)S(1)}, u32[]{:S(2)}, u32[]{:S(2)}) collective-permute-start(f32[8,10,3,8]{3,2,1,0:T(4,128)S(1)} %get-tuple-element.93), channel_id=1, source_target_pairs={{0,1},{1,2},{2,3},{3,4},{4,5},{5,6},{6,7},{8,9},{9,10},{10,11},{11... | collective-permute-start | bytes 23048 | tf_op jit(solution)/shard_map/ppermute | solution.py:21
  74.5 8.1 %collective-permute-start.30 = (f32[8,10,3,8]{3,2,1,0:T(4,128)S(1)}, f32[8,10,3,8]{3,2,1,0:T(4,128)S(1)}, u32[]{:S(2)}, u32[]{:S(2)}) collective-permute-start(f32[8,10,3,8]{3,2,1,0:T(4,128)S(1)} %get-tuple-element.92), channel_id=1, source_target_pairs={{1,0},{2,1},{3,2},{4,3},{5,4},{6,5},{7,6},{9,8},{10,9},{11,10},{12... | collective-permute-start | bytes 23048 | tf_op jit(solution)/shard_map/ppermute | solution.py:23
  85.2 28.6 %collective-permute-start.5 = (f32[5,3,8,8]{3,2,1,0:T(8,128)S(1)}, f32[5,3,8,8]{3,2,1,0:T(8,128)S(1)}, u32[]{:S(2)}, u32[]{:S(2)}) collective-permute-start(f32[5,3,8,8]{3,2,1,0:T(8,128)S(1)} %get-tuple-element.264), channel_id=1, source_target_pairs={{0,8},{8,16},{16,24},{1,9},{9,17},{17,25},{2,10},{10,18},{18,26},{... | collective-permute-start | bytes 11528 | tf_op jit(solution)/shard_map/ppermute | solution.py:21
  88.4 25.4 %collective-permute-start.4 = (f32[5,3,8,8]{3,2,1,0:T(8,128)S(1)}, f32[5,3,8,8]{3,2,1,0:T(8,128)S(1)}, u32[]{:S(2)}, u32[]{:S(2)}) collective-permute-start(f32[5,3,8,8]{3,2,1,0:T(8,128)S(1)} %get-tuple-element.265), channel_id=1, source_target_pairs={{8,0},{16,8},{24,16},{9,1},{17,9},{25,17},{10,2},{18,10},{26,18},{... | collective-permute-start | bytes 11528 | tf_op jit(solution)/shard_map/ppermute | solution.py:23
  89.7 30.3 %collective-permute-start.40 = (f32[8,3,8,8]{3,2,1,0:T(8,128)S(1)}, f32[8,3,8,8]{3,2,1,0:T(8,128)S(1)}, u32[]{:S(2)}, u32[]{:S(2)}) collective-permute-start(f32[8,3,8,8]{3,2,1,0:T(8,128)S(1)} %get-tuple-element.192), channel_id=1, source_target_pairs={{8,0},{16,8},{24,16},{9,1},{17,9},{25,17},{10,2},{18,10},{26,18},{... | collective-permute-start | bytes 18440 | tf_op jit(solution)/shard_map/ppermute | solution.py:23
  91.1 8.9 %collective-permute-start.33 = (bf16[5,1,8,8]{3,2,1,0:T(8,128)(2,1)S(1)}, bf16[5,1,8,8]{3,2,1,0:T(8,128)(2,1)S(1)}, u32[]{:S(2)}, u32[]{:S(2)}) collective-permute-start(bf16[5,1,8,8]{3,2,1,0:T(8,128)(2,1)S(1)} %get-tuple-element.303), channel_id=1, source_target_pairs={{8,0},{16,8},{24,16},{9,1},{17,9},{25,17},{10,2},{18,10},{26,18},{... | collective-permute-start | bytes 1928 | tf_op jit(solution)/shard_map/ppermute | solution.py:23
  92.4 7.9 %collective-permute-start.32 = (bf16[5,1,8,8]{3,2,1,0:T(8,128)(2,1)S(1)}, bf16[5,1,8,8]{3,2,1,0:T(8,128)(2,1)S(1)}, u32[]{:S(2)}, u32[]{:S(2)}) collective-permute-start(bf16[5,1,8,8]{3,2,1,0:T(8,128)(2,1)S(1)} %get-tuple-element.302), channel_id=1, source_target_pairs={{0,8},{8,16},{16,24},{1,9},{9,17},{17,25},{2,10},{10,18},{18,26},{... | collective-permute-start | bytes 1928 | tf_op jit(solution)/shard_map/ppermute | solution.py:21
  101.6 9.4 %collective-permute-start.34 = (bf16[5,6,1,8]{3,2,1,0:T(2,128)(2,1)S(1)}, bf16[5,6,1,8]{3,2,1,0:T(2,128)(2,1)S(1)}, u32[]{:S(2)}, u32[]{:S(2)}) collective-permute-start(bf16[5,6,1,8]{3,2,1,0:T(2,128)(2,1)S(1)} %get-tuple-element.284), channel_id=1, source_target_pairs={{0,1},{1,2},{2,3},{3,4},{4,5},{5,6},{6,7},{8,9},{9,10},{10,11},{11... | collective-permute-start | bytes 1448 | tf_op jit(solution)/shard_map/ppermute | solution.py:21
  107.7 12.3 %collective-permute-start.41 = (f32[8,3,8,8]{3,2,1,0:T(8,128)S(1)}, f32[8,3,8,8]{3,2,1,0:T(8,128)S(1)}, u32[]{:S(2)}, u32[]{:S(2)}) collective-permute-start(f32[8,3,8,8]{3,2,1,0:T(8,128)S(1)} %get-tuple-element.191), channel_id=1, source_target_pairs={{0,8},{8,16},{16,24},{1,9},{9,17},{17,25},{2,10},{10,18},{18,26},{... | collective-permute-start | bytes 18440 | tf_op jit(solution)/shard_map/ppermute | solution.py:21
  113.8 12.2 %collective-permute-start.7 = (f32[5,10,3,8]{3,2,1,0:T(4,128)S(1)}, f32[5,10,3,8]{3,2,1,0:T(4,128)S(1)}, u32[]{:S(2)}, u32[]{:S(2)}) collective-permute-start(f32[5,10,3,8]{3,2,1,0:T(4,128)S(1)} %get-tuple-element.149), channel_id=1, source_target_pairs={{0,1},{1,2},{2,3},{3,4},{4,5},{5,6},{6,7},{8,9},{9,10},{10,11},{11... | collective-permute-start | bytes 14408 | tf_op jit(solution)/shard_map/ppermute | solution.py:21
  118.4 7.7 %collective-permute-start.6 = (f32[5,10,3,8]{3,2,1,0:T(4,128)S(1)}, f32[5,10,3,8]{3,2,1,0:T(4,128)S(1)}, u32[]{:S(2)}, u32[]{:S(2)}) collective-permute-start(f32[5,10,3,8]{3,2,1,0:T(4,128)S(1)} %get-tuple-element.148), channel_id=1, source_target_pairs={{1,0},{2,1},{3,2},{4,3},{5,4},{6,5},{7,6},{9,8},{10,9},{11,10},{12... | collective-permute-start | bytes 14408 | tf_op jit(solution)/shard_map/ppermute | solution.py:23
  120.1 20.9 %collective-permute-start.43 = (f32[8,10,3,8]{3,2,1,0:T(4,128)S(1)}, f32[8,10,3,8]{3,2,1,0:T(4,128)S(1)}, u32[]{:S(2)}, u32[]{:S(2)}) collective-permute-start(f32[8,10,3,8]{3,2,1,0:T(4,128)S(1)} %get-tuple-element.91), channel_id=1, source_target_pairs={{0,1},{1,2},{2,3},{3,4},{4,5},{5,6},{6,7},{8,9},{9,10},{10,11},{11... | collective-permute-start | bytes 23048 | tf_op jit(solution)/shard_map/ppermute | solution.py:21
  124.7 16.3 %collective-permute-start.42 = (f32[8,10,3,8]{3,2,1,0:T(4,128)S(1)}, f32[8,10,3,8]{3,2,1,0:T(4,128)S(1)}, u32[]{:S(2)}, u32[]{:S(2)}) collective-permute-start(f32[8,10,3,8]{3,2,1,0:T(4,128)S(1)} %get-tuple-element.90), channel_id=1, source_target_pairs={{1,0},{2,1},{3,2},{4,3},{5,4},{6,5},{7,6},{9,8},{10,9},{11,10},{12... | collective-permute-start | bytes 23048 | tf_op jit(solution)/shard_map/ppermute | solution.py:23
  133.9 7.7 %collective-permute-start.11 = (f32[5,10,3,8]{3,2,1,0:T(4,128)S(1)}, f32[5,10,3,8]{3,2,1,0:T(4,128)S(1)}, u32[]{:S(2)}, u32[]{:S(2)}) collective-permute-start(f32[5,10,3,8]{3,2,1,0:T(4,128)S(1)} %get-tuple-element.147), channel_id=1, source_target_pairs={{0,1},{1,2},{2,3},{3,4},{4,5},{5,6},{6,7},{8,9},{9,10},{10,11},{11... | collective-permute-start | bytes 14408 | tf_op jit(solution)/shard_map/ppermute | solution.py:21
  139.4 7.5 %collective-permute-start.10 = (f32[5,10,3,8]{3,2,1,0:T(4,128)S(1)}, f32[5,10,3,8]{3,2,1,0:T(4,128)S(1)}, u32[]{:S(2)}, u32[]{:S(2)}) collective-permute-start(f32[5,10,3,8]{3,2,1,0:T(4,128)S(1)} %get-tuple-element.146), channel_id=1, source_target_pairs={{1,0},{2,1},{3,2},{4,3},{5,4},{6,5},{7,6},{9,8},{10,9},{11,10},{12... | collective-permute-start | bytes 14408 | tf_op jit(solution)/shard_map/ppermute | solution.py:23
  155.3 11.4 %collective-permute-start.15 = (f32[5,10,3,8]{3,2,1,0:T(4,128)S(1)}, f32[5,10,3,8]{3,2,1,0:T(4,128)S(1)}, u32[]{:S(2)}, u32[]{:S(2)}) collective-permute-start(f32[5,10,3,8]{3,2,1,0:T(4,128)S(1)} %get-tuple-element.145), channel_id=1, source_target_pairs={{0,1},{1,2},{2,3},{3,4},{4,5},{5,6},{6,7},{8,9},{9,10},{10,11},{11... | collective-permute-start | bytes 14408 | tf_op jit(solution)/shard_map/ppermute | solution.py:21
  180.0 24.7 %collective-permute-start.37 = (bf16[64,1,8,8]{0,3,2,1:T(8,128)(2,1)S(1)}, bf16[64,1,8,8]{0,3,2,1:T(8,128)(2,1)S(1)}, u32[]{:S(2)}, u32[]{:S(2)}) collective-permute-start(bf16[64,1,8,8]{0,3,2,1:T(8,128)(2,1)S(1)} %get-tuple-element.281), channel_id=1, source_target_pairs={{8,0},{16,8},{24,16},{9,1},{17,9},{25,17},{10,2},{18,10},{26,18},{... | collective-permute-start | bytes 24584 | tf_op jit(solution)/shard_map/ppermute | solution.py:23
  181.3 23.4 %collective-permute-start.36 = (bf16[64,1,8,8]{0,3,2,1:T(8,128)(2,1)S(1)}, bf16[64,1,8,8]{0,3,2,1:T(8,128)(2,1)S(1)}, u32[]{:S(2)}, u32[]{:S(2)}) collective-permute-start(bf16[64,1,8,8]{0,3,2,1:T(8,128)(2,1)S(1)} %get-tuple-element.280), channel_id=1, source_target_pairs={{0,8},{8,16},{16,24},{1,9},{9,17},{17,25},{2,10},{10,18},{18,26},{... | collective-permute-start | bytes 24584 | tf_op jit(solution)/shard_map/ppermute | solution.py:21
  205.4 7.6 %collective-permute-start.39 = (bf16[64,6,1,8]{0,3,2,1:T(8,128)(2,1)S(1)}, bf16[64,6,1,8]{0,3,2,1:T(8,128)(2,1)S(1)}, u32[]{:S(2)}, u32[]{:S(2)}) collective-permute-start(bf16[64,6,1,8]{0,3,2,1:T(8,128)(2,1)S(1)} %get-tuple-element.228), channel_id=1, source_target_pairs={{1,0},{2,1},{3,2},{4,3},{5,4},{6,5},{7,6},{9,8},{10,9},{11,10},{12... | collective-permute-start | bytes 18440 | tf_op jit(solution)/shard_map/ppermute | solution.py:23
  214.1 17.3 %collective-permute-start.45 = (bf16[64,1,8,8]{0,3,2,1:T(8,128)(2,1)S(1)}, bf16[64,1,8,8]{0,3,2,1:T(8,128)(2,1)S(1)}, u32[]{:S(2)}, u32[]{:S(2)}) collective-permute-start(bf16[64,1,8,8]{0,3,2,1:T(8,128)(2,1)S(1)} %get-tuple-element.279), channel_id=1, source_target_pairs={{8,0},{16,8},{24,16},{9,1},{17,9},{25,17},{10,2},{18,10},{26,18},{... | collective-permute-start | bytes 24584 | tf_op jit(solution)/shard_map/ppermute | solution.py:23
  215.4 16.0 %collective-permute-start.44 = (bf16[64,1,8,8]{0,3,2,1:T(8,128)(2,1)S(1)}, bf16[64,1,8,8]{0,3,2,1:T(8,128)(2,1)S(1)}, u32[]{:S(2)}, u32[]{:S(2)}) collective-permute-start(bf16[64,1,8,8]{0,3,2,1:T(8,128)(2,1)S(1)} %get-tuple-element.278), channel_id=1, source_target_pairs={{0,8},{8,16},{16,24},{1,9},{9,17},{17,25},{2,10},{10,18},{18,26},{... | collective-permute-start | bytes 24584 | tf_op jit(solution)/shard_map/ppermute | solution.py:21
  249.0 7.7 %collective-permute-start.51 = (f32[8,10,3,8]{3,2,1,0:T(4,128)S(1)}, f32[8,10,3,8]{3,2,1,0:T(4,128)S(1)}, u32[]{:S(2)}, u32[]{:S(2)}) collective-permute-start(f32[8,10,3,8]{3,2,1,0:T(4,128)S(1)} %get-tuple-element.89), channel_id=1, source_target_pairs={{0,1},{1,2},{2,3},{3,4},{4,5},{5,6},{6,7},{8,9},{9,10},{10,11},{11... | collective-permute-start | bytes 23048 | tf_op jit(solution)/shard_map/ppermute | solution.py:21
  253.5 8.4 %collective-permute-start.50 = (f32[8,10,3,8]{3,2,1,0:T(4,128)S(1)}, f32[8,10,3,8]{3,2,1,0:T(4,128)S(1)}, u32[]{:S(2)}, u32[]{:S(2)}) collective-permute-start(f32[8,10,3,8]{3,2,1,0:T(4,128)S(1)} %get-tuple-element.88), channel_id=1, source_target_pairs={{1,0},{2,1},{3,2},{4,3},{5,4},{6,5},{7,6},{9,8},{10,9},{11,10},{12... | collective-permute-start | bytes 23048 | tf_op jit(solution)/shard_map/ppermute | solution.py:23
  263.9 19.7 %collective-permute-start.52 = (f32[8,3,8,8]{3,2,1,0:T(8,128)S(1)}, f32[8,3,8,8]{3,2,1,0:T(8,128)S(1)}, u32[]{:S(2)}, u32[]{:S(2)}) collective-permute-start(f32[8,3,8,8]{3,2,1,0:T(8,128)S(1)} %get-tuple-element.182), channel_id=1, source_target_pairs={{8,0},{16,8},{24,16},{9,1},{17,9},{25,17},{10,2},{18,10},{26,18},{... | collective-permute-start | bytes 18440 | tf_op jit(solution)/shard_map/ppermute | solution.py:23
  265.2 18.4 %collective-permute-start.53 = (f32[8,3,8,8]{3,2,1,0:T(8,128)S(1)}, f32[8,3,8,8]{3,2,1,0:T(8,128)S(1)}, u32[]{:S(2)}, u32[]{:S(2)}) collective-permute-start(f32[8,3,8,8]{3,2,1,0:T(8,128)S(1)} %get-tuple-element.181), channel_id=1, source_target_pairs={{0,8},{8,16},{16,24},{1,9},{9,17},{17,25},{2,10},{10,18},{18,26},{... | collective-permute-start | bytes 18440 | tf_op jit(solution)/shard_map/ppermute | solution.py:21
  269.0 6.9 %collective-permute-start.17 = (f32[5,3,8,8]{3,2,1,0:T(8,128)S(1)}, f32[5,3,8,8]{3,2,1,0:T(8,128)S(1)}, u32[]{:S(2)}, u32[]{:S(2)}) collective-permute-start(f32[5,3,8,8]{3,2,1,0:T(8,128)S(1)} %get-tuple-element.246), channel_id=1, source_target_pairs={{0,8},{8,16},{16,24},{1,9},{9,17},{17,25},{2,10},{10,18},{18,26},{... | collective-permute-start | bytes 11528 | tf_op jit(solution)/shard_map/ppermute | solution.py:21
  277.2 13.1 %collective-permute-start.19 = (f32[5,10,3,8]{3,2,1,0:T(4,128)S(1)}, f32[5,10,3,8]{3,2,1,0:T(4,128)S(1)}, u32[]{:S(2)}, u32[]{:S(2)}) collective-permute-start(f32[5,10,3,8]{3,2,1,0:T(4,128)S(1)} %get-tuple-element.141), channel_id=1, source_target_pairs={{0,1},{1,2},{2,3},{3,4},{4,5},{5,6},{6,7},{8,9},{9,10},{10,11},{11... | collective-permute-start | bytes 14408 | tf_op jit(solution)/shard_map/ppermute | solution.py:21
  282.0 8.3 %collective-permute-start.18 = (f32[5,10,3,8]{3,2,1,0:T(4,128)S(1)}, f32[5,10,3,8]{3,2,1,0:T(4,128)S(1)}, u32[]{:S(2)}, u32[]{:S(2)}) collective-permute-start(f32[5,10,3,8]{3,2,1,0:T(4,128)S(1)} %get-tuple-element.140), channel_id=1, source_target_pairs={{1,0},{2,1},{3,2},{4,3},{5,4},{6,5},{7,6},{9,8},{10,9},{11,10},{12... | collective-permute-start | bytes 14408 | tf_op jit(solution)/shard_map/ppermute | solution.py:23
  283.7 7.8 %collective-permute-start.55 = (f32[8,10,3,8]{3,2,1,0:T(4,128)S(1)}, f32[8,10,3,8]{3,2,1,0:T(4,128)}, u32[]{:S(2)}, u32[]{:S(2)}) collective-permute-start(f32[8,10,3,8]{3,2,1,0:T(4,128)S(1)} %get-tuple-element.87), channel_id=1, source_target_pairs={{0,1},{1,2},{2,3},{3,4},{4,5},{5,6},{6,7},{8,9},{9,10},{10,11},{11... | collective-permute-start | bytes 23048 | tf_op jit(solution)/shard_map/ppermute | solution.py:21
  288.9 8.0 %collective-permute-start.54 = (f32[8,10,3,8]{3,2,1,0:T(4,128)S(1)}, f32[8,10,3,8]{3,2,1,0:T(4,128)}, u32[]{:S(2)}, u32[]{:S(2)}) collective-permute-start(f32[8,10,3,8]{3,2,1,0:T(4,128)S(1)} %get-tuple-element.86), channel_id=1, source_target_pairs={{1,0},{2,1},{3,2},{4,3},{5,4},{6,5},{7,6},{9,8},{10,9},{11,10},{12... | collective-permute-start | bytes 23048 | tf_op jit(solution)/shard_map/ppermute | solution.py:23
  299.9 71.5 %collective-permute-start.21 = (f32[5,3,8,8]{3,2,1,0:T(8,128)}, f32[5,3,8,8]{3,2,1,0:T(8,128)S(1)}, u32[]{:S(2)}, u32[]{:S(2)}) collective-permute-start(f32[5,3,8,8]{3,2,1,0:T(8,128)} %get-tuple-element.243), channel_id=1, source_target_pairs={{0,8},{8,16},{16,24},{1,9},{9,17},{17,25},{2,10},{10,18},{18,26},{... | collective-permute-start | bytes 11528 | tf_op jit(solution)/shard_map/ppermute | solution.py:21
  302.7 68.7 %collective-permute-start.20 = (f32[5,3,8,8]{3,2,1,0:T(8,128)}, f32[5,3,8,8]{3,2,1,0:T(8,128)S(1)}, u32[]{:S(2)}, u32[]{:S(2)}) collective-permute-start(f32[5,3,8,8]{3,2,1,0:T(8,128)} %get-tuple-element.242), channel_id=1, source_target_pairs={{8,0},{16,8},{24,16},{9,1},{17,9},{25,17},{10,2},{18,10},{26,18},{... | collective-permute-start | bytes 11528 | tf_op jit(solution)/shard_map/ppermute | solution.py:23
  304.3 13.8 %collective-permute-start.57 = (bf16[5,1,8,8]{3,2,1,0:T(8,128)(2,1)S(1)}, bf16[5,1,8,8]{3,2,1,0:T(8,128)(2,1)S(1)}, u32[]{:S(2)}, u32[]{:S(2)}) collective-permute-start(bf16[5,1,8,8]{3,2,1,0:T(8,128)(2,1)S(1)} %get-tuple-element.301), channel_id=1, source_target_pairs={{8,0},{16,8},{24,16},{9,1},{17,9},{25,17},{10,2},{18,10},{26,18},{... | collective-permute-start | bytes 1928 | tf_op jit(solution)/shard_map/ppermute | solution.py:23
  305.6 12.5 %collective-permute-start.56 = (bf16[5,1,8,8]{3,2,1,0:T(8,128)(2,1)S(1)}, bf16[5,1,8,8]{3,2,1,0:T(8,128)(2,1)S(1)}, u32[]{:S(2)}, u32[]{:S(2)}) collective-permute-start(bf16[5,1,8,8]{3,2,1,0:T(8,128)(2,1)S(1)} %get-tuple-element.300), channel_id=1, source_target_pairs={{0,8},{8,16},{16,24},{1,9},{9,17},{17,25},{2,10},{10,18},{18,26},{... | collective-permute-start | bytes 1928 | tf_op jit(solution)/shard_map/ppermute | solution.py:21
  328.2 10.7 %collective-permute-start.61 = (bf16[64,1,8,8]{0,3,2,1:T(8,128)(2,1)S(1)}, bf16[64,1,8,8]{0,3,2,1:T(8,128)(2,1)S(1)}, u32[]{:S(2)}, u32[]{:S(2)}) collective-permute-start(bf16[64,1,8,8]{0,3,2,1:T(8,128)(2,1)S(1)} %get-tuple-element.277), channel_id=1, source_target_pairs={{8,0},{16,8},{24,16},{9,1},{17,9},{25,17},{10,2},{18,10},{26,18},{... | collective-permute-start | bytes 24584 | tf_op jit(solution)/shard_map/ppermute | solution.py:23
  329.5 9.4 %collective-permute-start.60 = (bf16[64,1,8,8]{0,3,2,1:T(8,128)(2,1)S(1)}, bf16[64,1,8,8]{0,3,2,1:T(8,128)(2,1)S(1)}, u32[]{:S(2)}, u32[]{:S(2)}) collective-permute-start(bf16[64,1,8,8]{0,3,2,1:T(8,128)(2,1)S(1)} %get-tuple-element.276), channel_id=1, source_target_pairs={{0,8},{8,16},{16,24},{1,9},{9,17},{17,25},{2,10},{10,18},{18,26},{... | collective-permute-start | bytes 24584 | tf_op jit(solution)/shard_map/ppermute | solution.py:21
  369.3 263.5 %all-reduce.4.cloned.1.call-start = ((), (), s32[]{:S(2)}) async-start(), calls=%async_computation | async-start | bytes 1769472 | tf_op jit(solution)/shard_map/psum | solution.py:266
  371.5 8.2 %collective-permute-start.23 = (f32[5,10,3,8]{3,2,1,0:T(4,128)S(1)}, f32[5,10,3,8]{3,2,1,0:T(4,128)S(1)}, u32[]{:S(2)}, u32[]{:S(2)}) collective-permute-start(f32[5,10,3,8]{3,2,1,0:T(4,128)S(1)} %get-tuple-element.139), channel_id=1, source_target_pairs={{0,1},{1,2},{2,3},{3,4},{4,5},{5,6},{6,7},{8,9},{9,10},{10,11},{11... | collective-permute-start | bytes 14408 | tf_op jit(solution)/shard_map/ppermute | solution.py:21
  376.5 8.5 %collective-permute-start.22 = (f32[5,10,3,8]{3,2,1,0:T(4,128)S(1)}, f32[5,10,3,8]{3,2,1,0:T(4,128)S(1)}, u32[]{:S(2)}, u32[]{:S(2)}) collective-permute-start(f32[5,10,3,8]{3,2,1,0:T(4,128)S(1)} %get-tuple-element.138), channel_id=1, source_target_pairs={{1,0},{2,1},{3,2},{4,3},{5,4},{6,5},{7,6},{9,8},{10,9},{11,10},{12... | collective-permute-start | bytes 14408 | tf_op jit(solution)/shard_map/ppermute | solution.py:23
  (124 other events, 439.2 us)
Sparse Core Ops, SparseCore 0:
  369.4 128.6 all-reduce.5
  503.3 129.3 all-reduce.3
where the time goes:
time: 652 us; the launch traced here: 643 us
  waiting for transfers between devices  289 us (44%)
  starting transfers between devices  182 us (28%)
  local copies, waits for them, and re-layouts  68.4 us (10%)
  matrix products  65.6 us (10%)
  other arithmetic  20.1 us (3%)
  between operations  17.5 us (3%)
    psum x2, waiting for transfers between devices, body(): result = lax.psum((totals[0], totals[1], totals[2]), ('gx', 'gy'))  244 us
    ppermute x32, starting transfers between devices, padded_2(): lax.ppermute(tail, axis, [(i, (i + 1) % count) for i in range(ends)])  140 us
    ppermute x32, starting transfers between devices, padded_2(): lax.ppermute(head, axis, [((i + 1) % count, i) for i in range(ends)])  41.7 us
    unnamed x240, local copies, waits for them, and re-layouts  40.9 us
    dot_general x162, matrix products, kernel_grad(): lax.dot_general(flat_grad, window.reshape(channels, -1), (((1,), (1,)), (...  37 us
    ppermute x32, waiting for transfers between devices, padded_2(): lax.ppermute(head, axis, [((i + 1) % count, i) for i in range(ends)])  35.6 us
    conv_general_dilated x11, matrix products, conv_valid(): lax.conv_general_dilated(padded[None], kernel, (1, 1, 1), 'VALID', dimens...  28.6 us
  transfers between devices with their start and end apart: 66, of which 22 were waited for; matrix products, arithmetic and copies ran while one was open for 14% of the time, Pallas kernels for 0%

commit v1 on v0

--- a/solution.py
+++ b/solution.py
@@ -263,7 +263,8 @@
         )
         if step_index > 0:
             adjoint_in = carried + state_grad
-    result = lax.psum((totals[0], totals[1], totals[2]), ("gx", "gy"))
+    half = lax.psum((totals[0], totals[1], totals[2]), "gx")
+    result = lax.psum(half, "gy")
     return (current.reshape(channels, size_x, size_y * NZ), result[0], result[1], result[2])
 
 

time: 652 us -> 616 us (0.945)
  waiting for transfers between devices: 289 us -> 253 us
    psum x2 -> x4, waiting for transfers between devices: 244 us -> 208 us  [the longest x2 150 us: body(): result = lax.psum(half, 'gy')]
  transfers between devices with their start and end apart: 66 -> 68, of which waited for: 22 -> 24; matrix products, arithmetic and copies ran while one was open for 14% -> 15% of each run, Pallas kernels for 0% -> 0%
where the time goes in v1:
time: 616 us; the launch traced here: 606 us
  waiting for transfers between devices  253 us (41%)
  starting transfers between devices  182 us (30%)
  local copies, waits for them, and re-layouts  68.5 us (11%)
  matrix products  65.6 us (11%)
  other arithmetic  20.1 us (3%)
  between operations  17.2 us (3%)
    psum x2, waiting for transfers between devices, body(): result = lax.psum(half, 'gy')  150 us
    ppermute x32, starting transfers between devices, padded_2(): lax.ppermute(tail, axis, [(i, (i + 1) % count) for i in range(ends)])  140 us
    psum x2, waiting for transfers between devices, body(): half = lax.psum((totals[0], totals[1], totals[2]), 'gx')  58.1 us
    ppermute x32, starting transfers between devices, padded_2(): lax.ppermute(head, axis, [((i + 1) % count, i) for i in range(ends)])  41.7 us
    unnamed x240, local copies, waits for them, and re-layouts  41 us
    dot_general x162, matrix products, kernel_grad(): lax.dot_general(flat_grad, window.reshape(channels, -1), (((1,), (1,)), (...  37 us
    ppermute x32, waiting for transfers between devices, padded_2(): lax.ppermute(head, axis, [((i + 1) % count, i) for i in range(ends)])  35.6 us
    conv_general_dilated x11, matrix products, conv_valid(): lax.conv_general_dilated(padded[None], kernel, (1, 1, 1), 'VALID', dimens...  28.6 us
  transfers between devices with their start and end apart: 68, of which 24 were waited for; matrix products, arithmetic and copies ran while one was open for 15% of the time, Pallas kernels for 0%

profile of v1, /device:TPU:0, one launch (start us, length us, event | category | flops | bytes accessed | tf_op | source)
XLA Modules:
  0.0 606.3 jit_solution(10952548684228454874)
XLA Ops:
  14.4 5.8 collective-permute-start.25
  30.3 3.4 collective-permute-start.3
  35.9 5.2 collective-permute-start.27
  46.2 2.5 convolution_tanh_fusion
  49.9 5.2 fusion.164
  58.3 2.8 fusion.175
  65.7 3.4 collective-permute-start.29
  70.2 4.3 collective-permute-start.31
  77.6 5.0 collective-permute-done.30
  85.1 3.2 collective-permute-start.5
  92.4 7.0 %collective-permute-start.32 = (bf16[5,1,8,8]{3,2,1,0:T(8,128)(2,1)S(1)}, bf16[5,1,8,8]{3,2,1,0:T(8,128)(2,1)S(1)}, u32[]{:S(2)}, u32[]{:S(2)}) collective-permute-start(bf16[5,1,8,8]{3,2,1,0:T(8,128)(2,1)S(1)} %get-tuple-element.304), channel_id=1, source_target_pairs={{0,8},{8,16},{16,24},{1,9},{9,17},{17,25},{2,10},{10,18},{18,26},{... | collective-permute-start | bytes 1928 | tf_op jit(solution)/shard_map/ppermute | solution.py:21
  101.6 5.4 collective-permute-start.34
  107.7 3.3 collective-permute-start.41
  113.8 4.5 collective-permute-start.7
  120.1 4.6 collective-permute-start.43
  126.4 3.9 collective-permute-start.9
  133.9 5.4 collective-permute-start.11
  141.6 5.2 collective-permute-done.10
  147.8 3.7 collective-permute-start.13
  155.3 4.8 collective-permute-start.15
  162.4 4.3 collective-permute-done.14
  170.8 2.5 fusion.691
  174.6 5.2 fusion.162
  181.3 4.2 collective-permute-start.36
  186.6 2.8 fusion.173
  206.7 4.5 collective-permute-start.38
  215.4 3.7 collective-permute-start.44
  232.7 5.0 collective-permute-start.46
  239.0 2.8 fusion.171
  244.2 3.7 collective-permute-start.49
  249.0 4.5 collective-permute-start.51
  256.6 5.3 collective-permute-done.50
  265.2 3.6 collective-permute-start.53
  269.0 5.0 collective-permute-start.17
  277.1 4.8 collective-permute-start.19
  283.7 5.2 collective-permute-start.55
  291.5 5.4 collective-permute-done.54
  299.9 2.8 collective-permute-start.21
  305.6 4.4 collective-permute-start.56
  319.4 4.5 collective-permute-start.58
  329.4 3.5 collective-permute-start.60
  340.2 4.7 collective-permute-start.62
  371.6 4.9 collective-permute-start.23
  379.6 5.3 collective-permute-done.22
  385.5 20.1 %all-reduce.13.cloned.1.call-done = (f32[64,135]{0,1:T(8,128)}, f32[5,1728]{1,0:T(8,128)}) async-done(((f32[64,135]{0,1:T(8,128)}, f32[5,1728]{1,0:T(8,128)}), (f32[64,135]{0,1:T(8,128)}, f32[5,1728]{1,0:T(8,128)})) %all-reduce.13.cloned.1.call-update) | async-done | bytes 69136 | tf_op jit(solution)/shard_map/psum | solution.py:266
  405.7 38.0 %all-reduce.7.cloned.1.call-done = f32[64,1728]{0,1:T(8,128)} async-done(((f32[64,1728]{0,1:T(8,128)}), f32[64,1728]{0,1:T(8,128)}) %all-reduce.7.cloned.1.call-update) | async-done | bytes 442384 | tf_op jit(solution)/shard_map/psum | solution.py:266
  445.1 72.2 %all-reduce.11.cloned.1.call-done = (f32[64,135]{0,1:T(8,128)}, f32[5,1728]{1,0:T(8,128)}) async-done(((f32[64,135]{0,1:T(8,128)}, f32[5,1728]{1,0:T(8,128)}), (f32[64,135]{0,1:T(8,128)}, f32[5,1728]{1,0:T(8,128)})) %all-reduce.11.cloned.1.call-update) | async-done | bytes 69136 | tf_op jit(solution)/shard_map/psum | solution.py:267
  518.9 77.7 %all-reduce.9.cloned.1.call-done = f32[64,1728]{0,1:T(8,128)} async-done(((f32[64,1728]{0,1:T(8,128)}), f32[64,1728]{0,1:T(8,128)}) %all-reduce.9.cloned.1.call-update) | async-done | bytes 442384 | tf_op jit(solution)/shard_map/psum | solution.py:267
  (805 shorter events, 189.2 us)
Async XLA Ops:
  7.2 398.5 %all-reduce.13.cloned.1.call-start = ((), (), s32[]{:S(2)}) async-start(), calls=%async_computation.3 | async-start | bytes 253952 | tf_op jit(solution)/shard_map/psum | solution.py:266
  8.0 21.2 %collective-permute-start.1 = (f32[5,3,8,8]{3,2,1,0:T(8,128)S(1)}, f32[5,3,8,8]{3,2,1,0:T(8,128)S(1)}, u32[]{:S(2)}, u32[]{:S(2)}) collective-permute-start(f32[5,3,8,8]{3,2,1,0:T(8,128)S(1)} %get-tuple-element.275), channel_id=1, source_target_pairs={{0,8},{8,16},{16,24},{1,9},{9,17},{17,25},{2,10},{10,18},{18,26},{... | collective-permute-start | bytes 11528 | tf_op jit(solution)/shard_map/ppermute | solution.py:21
  10.5 19.8 %collective-permute-start = (f32[5,3,8,8]{3,2,1,0:T(8,128)S(1)}, f32[5,3,8,8]{3,2,1,0:T(8,128)S(1)}, u32[]{:S(2)}, u32[]{:S(2)}) collective-permute-start(f32[5,3,8,8]{3,2,1,0:T(8,128)S(1)} %get-tuple-element.274), channel_id=1, source_target_pairs={{8,0},{16,8},{24,16},{9,1},{17,9},{25,17},{10,2},{18,10},{26,18},{... | collective-permute-start | bytes 11528 | tf_op jit(solution)/shard_map/ppermute | solution.py:23
  13.1 21.9 %collective-permute-start.24 = (f32[8,3,8,8]{3,2,1,0:T(8,128)S(1)}, f32[8,3,8,8]{3,2,1,0:T(8,128)S(1)}, u32[]{:S(2)}, u32[]{:S(2)}) collective-permute-start(f32[8,3,8,8]{3,2,1,0:T(8,128)S(1)} %get-tuple-element.204), channel_id=1, source_target_pairs={{8,0},{16,8},{24,16},{9,1},{17,9},{25,17},{10,2},{18,10},{26,18},{... | collective-permute-start | bytes 18440 | tf_op jit(solution)/shard_map/ppermute | solution.py:23
  14.4 20.6 %collective-permute-start.25 = (f32[8,3,8,8]{3,2,1,0:T(8,128)S(1)}, f32[8,3,8,8]{3,2,1,0:T(8,128)S(1)}, u32[]{:S(2)}, u32[]{:S(2)}) collective-permute-start(f32[8,3,8,8]{3,2,1,0:T(8,128)S(1)} %get-tuple-element.203), channel_id=1, source_target_pairs={{0,8},{8,16},{16,24},{1,9},{9,17},{17,25},{2,10},{10,18},{18,26},{... | collective-permute-start | bytes 18440 | tf_op jit(solution)/shard_map/ppermute | solution.py:21
  30.3 12.2 %collective-permute-start.3 = (f32[5,10,3,8]{3,2,1,0:T(4,128)S(1)}, f32[5,10,3,8]{3,2,1,0:T(4,128)S(1)}, u32[]{:S(2)}, u32[]{:S(2)}) collective-permute-start(f32[5,10,3,8]{3,2,1,0:T(4,128)S(1)} %get-tuple-element.155), channel_id=1, source_target_pairs={{0,1},{1,2},{2,3},{3,4},{4,5},{5,6},{6,7},{8,9},{9,10},{10,11},{11... | collective-permute-start | bytes 14408 | tf_op jit(solution)/shard_map/ppermute | solution.py:21
  33.7 8.7 %collective-permute-start.2 = (f32[5,10,3,8]{3,2,1,0:T(4,128)S(1)}, f32[5,10,3,8]{3,2,1,0:T(4,128)S(1)}, u32[]{:S(2)}, u32[]{:S(2)}) collective-permute-start(f32[5,10,3,8]{3,2,1,0:T(4,128)S(1)} %get-tuple-element.154), channel_id=1, source_target_pairs={{1,0},{2,1},{3,2},{4,3},{5,4},{6,5},{7,6},{9,8},{10,9},{11,10},{12... | collective-permute-start | bytes 14408 | tf_op jit(solution)/shard_map/ppermute | solution.py:23
  35.9 27.0 %collective-permute-start.27 = (f32[8,10,3,8]{3,2,1,0:T(4,128)}, f32[8,10,3,8]{3,2,1,0:T(4,128)}, u32[]{:S(2)}, u32[]{:S(2)}) collective-permute-start(f32[8,10,3,8]{3,2,1,0:T(4,128)} %get-tuple-element.97), channel_id=1, source_target_pairs={{0,1},{1,2},{2,3},{3,4},{4,5},{5,6},{6,7},{8,9},{9,10},{10,11},{11... | collective-permute-start | bytes 23048 | tf_op jit(solution)/shard_map/ppermute | solution.py:21
  41.1 21.8 %collective-permute-start.26 = (f32[8,10,3,8]{3,2,1,0:T(4,128)}, f32[8,10,3,8]{3,2,1,0:T(4,128)}, u32[]{:S(2)}, u32[]{:S(2)}) collective-permute-start(f32[8,10,3,8]{3,2,1,0:T(4,128)} %get-tuple-element.96), channel_id=1, source_target_pairs={{1,0},{2,1},{3,2},{4,3},{5,4},{6,5},{7,6},{9,8},{10,9},{11,10},{12... | collective-permute-start | bytes 23048 | tf_op jit(solution)/shard_map/ppermute | solution.py:23
  74.5 8.1 %collective-permute-start.30 = (f32[8,10,3,8]{3,2,1,0:T(4,128)S(1)}, f32[8,10,3,8]{3,2,1,0:T(4,128)S(1)}, u32[]{:S(2)}, u32[]{:S(2)}) collective-permute-start(f32[8,10,3,8]{3,2,1,0:T(4,128)S(1)} %get-tuple-element.94), channel_id=1, source_target_pairs={{1,0},{2,1},{3,2},{4,3},{5,4},{6,5},{7,6},{9,8},{10,9},{11,10},{12... | collective-permute-start | bytes 23048 | tf_op jit(solution)/shard_map/ppermute | solution.py:23
  85.1 28.6 %collective-permute-start.5 = (f32[5,3,8,8]{3,2,1,0:T(8,128)S(1)}, f32[5,3,8,8]{3,2,1,0:T(8,128)S(1)}, u32[]{:S(2)}, u32[]{:S(2)}) collective-permute-start(f32[5,3,8,8]{3,2,1,0:T(8,128)S(1)} %get-tuple-element.266), channel_id=1, source_target_pairs={{0,8},{8,16},{16,24},{1,9},{9,17},{17,25},{2,10},{10,18},{18,26},{... | collective-permute-start | bytes 11528 | tf_op jit(solution)/shard_map/ppermute | solution.py:21
  88.4 25.4 %collective-permute-start.4 = (f32[5,3,8,8]{3,2,1,0:T(8,128)S(1)}, f32[5,3,8,8]{3,2,1,0:T(8,128)S(1)}, u32[]{:S(2)}, u32[]{:S(2)}) collective-permute-start(f32[5,3,8,8]{3,2,1,0:T(8,128)S(1)} %get-tuple-element.267), channel_id=1, source_target_pairs={{8,0},{16,8},{24,16},{9,1},{17,9},{25,17},{10,2},{18,10},{26,18},{... | collective-permute-start | bytes 11528 | tf_op jit(solution)/shard_map/ppermute | solution.py:23
  89.7 30.3 %collective-permute-start.40 = (f32[8,3,8,8]{3,2,1,0:T(8,128)S(1)}, f32[8,3,8,8]{3,2,1,0:T(8,128)S(1)}, u32[]{:S(2)}, u32[]{:S(2)}) collective-permute-start(f32[8,3,8,8]{3,2,1,0:T(8,128)S(1)} %get-tuple-element.194), channel_id=1, source_target_pairs={{8,0},{16,8},{24,16},{9,1},{17,9},{25,17},{10,2},{18,10},{26,18},{... | collective-permute-start | bytes 18440 | tf_op jit(solution)/shard_map/ppermute | solution.py:23
  91.1 8.9 %collective-permute-start.33 = (bf16[5,1,8,8]{3,2,1,0:T(8,128)(2,1)S(1)}, bf16[5,1,8,8]{3,2,1,0:T(8,128)(2,1)S(1)}, u32[]{:S(2)}, u32[]{:S(2)}) collective-permute-start(bf16[5,1,8,8]{3,2,1,0:T(8,128)(2,1)S(1)} %get-tuple-element.305), channel_id=1, source_target_pairs={{8,0},{16,8},{24,16},{9,1},{17,9},{25,17},{10,2},{18,10},{26,18},{... | collective-permute-start | bytes 1928 | tf_op jit(solution)/shard_map/ppermute | solution.py:23
  92.4 7.9 %collective-permute-start.32 = (bf16[5,1,8,8]{3,2,1,0:T(8,128)(2,1)S(1)}, bf16[5,1,8,8]{3,2,1,0:T(8,128)(2,1)S(1)}, u32[]{:S(2)}, u32[]{:S(2)}) collective-permute-start(bf16[5,1,8,8]{3,2,1,0:T(8,128)(2,1)S(1)} %get-tuple-element.304), channel_id=1, source_target_pairs={{0,8},{8,16},{16,24},{1,9},{9,17},{17,25},{2,10},{10,18},{18,26},{... | collective-permute-start | bytes 1928 | tf_op jit(solution)/shard_map/ppermute | solution.py:21
  101.6 9.4 %collective-permute-start.34 = (bf16[5,6,1,8]{3,2,1,0:T(2,128)(2,1)S(1)}, bf16[5,6,1,8]{3,2,1,0:T(2,128)(2,1)S(1)}, u32[]{:S(2)}, u32[]{:S(2)}) collective-permute-start(bf16[5,6,1,8]{3,2,1,0:T(2,128)(2,1)S(1)} %get-tuple-element.286), channel_id=1, source_target_pairs={{0,1},{1,2},{2,3},{3,4},{4,5},{5,6},{6,7},{8,9},{9,10},{10,11},{11... | collective-permute-start | bytes 1448 | tf_op jit(solution)/shard_map/ppermute | solution.py:21
  107.7 12.3 %collective-permute-start.41 = (f32[8,3,8,8]{3,2,1,0:T(8,128)S(1)}, f32[8,3,8,8]{3,2,1,0:T(8,128)S(1)}, u32[]{:S(2)}, u32[]{:S(2)}) collective-permute-start(f32[8,3,8,8]{3,2,1,0:T(8,128)S(1)} %get-tuple-element.193), channel_id=1, source_target_pairs={{0,8},{8,16},{16,24},{1,9},{9,17},{17,25},{2,10},{10,18},{18,26},{... | collective-permute-start | bytes 18440 | tf_op jit(solution)/shard_map/ppermute | solution.py:21
  113.8 12.2 %collective-permute-start.7 = (f32[5,10,3,8]{3,2,1,0:T(4,128)S(1)}, f32[5,10,3,8]{3,2,1,0:T(4,128)S(1)}, u32[]{:S(2)}, u32[]{:S(2)}) collective-permute-start(f32[5,10,3,8]{3,2,1,0:T(4,128)S(1)} %get-tuple-element.151), channel_id=1, source_target_pairs={{0,1},{1,2},{2,3},{3,4},{4,5},{5,6},{6,7},{8,9},{9,10},{10,11},{11... | collective-permute-start | bytes 14408 | tf_op jit(solution)/shard_map/ppermute | solution.py:21
  118.4 7.7 %collective-permute-start.6 = (f32[5,10,3,8]{3,2,1,0:T(4,128)S(1)}, f32[5,10,3,8]{3,2,1,0:T(4,128)S(1)}, u32[]{:S(2)}, u32[]{:S(2)}) collective-permute-start(f32[5,10,3,8]{3,2,1,0:T(4,128)S(1)} %get-tuple-element.150), channel_id=1, source_target_pairs={{1,0},{2,1},{3,2},{4,3},{5,4},{6,5},{7,6},{9,8},{10,9},{11,10},{12... | collective-permute-start | bytes 14408 | tf_op jit(solution)/shard_map/ppermute | solution.py:23
  120.1 20.9 %collective-permute-start.43 = (f32[8,10,3,8]{3,2,1,0:T(4,128)S(1)}, f32[8,10,3,8]{3,2,1,0:T(4,128)S(1)}, u32[]{:S(2)}, u32[]{:S(2)}) collective-permute-start(f32[8,10,3,8]{3,2,1,0:T(4,128)S(1)} %get-tuple-element.93), channel_id=1, source_target_pairs={{0,1},{1,2},{2,3},{3,4},{4,5},{5,6},{6,7},{8,9},{9,10},{10,11},{11... | collective-permute-start | bytes 23048 | tf_op jit(solution)/shard_map/ppermute | solution.py:21
  124.7 16.3 %collective-permute-start.42 = (f32[8,10,3,8]{3,2,1,0:T(4,128)S(1)}, f32[8,10,3,8]{3,2,1,0:T(4,128)S(1)}, u32[]{:S(2)}, u32[]{:S(2)}) collective-permute-start(f32[8,10,3,8]{3,2,1,0:T(4,128)S(1)} %get-tuple-element.92), channel_id=1, source_target_pairs={{1,0},{2,1},{3,2},{4,3},{5,4},{6,5},{7,6},{9,8},{10,9},{11,10},{12... | collective-permute-start | bytes 23048 | tf_op jit(solution)/shard_map/ppermute | solution.py:23
  133.9 7.7 %collective-permute-start.11 = (f32[5,10,3,8]{3,2,1,0:T(4,128)S(1)}, f32[5,10,3,8]{3,2,1,0:T(4,128)S(1)}, u32[]{:S(2)}, u32[]{:S(2)}) collective-permute-start(f32[5,10,3,8]{3,2,1,0:T(4,128)S(1)} %get-tuple-element.149), channel_id=1, source_target_pairs={{0,1},{1,2},{2,3},{3,4},{4,5},{5,6},{6,7},{8,9},{9,10},{10,11},{11... | collective-permute-start | bytes 14408 | tf_op jit(solution)/shard_map/ppermute | solution.py:21
  139.4 7.5 %collective-permute-start.10 = (f32[5,10,3,8]{3,2,1,0:T(4,128)S(1)}, f32[5,10,3,8]{3,2,1,0:T(4,128)S(1)}, u32[]{:S(2)}, u32[]{:S(2)}) collective-permute-start(f32[5,10,3,8]{3,2,1,0:T(4,128)S(1)} %get-tuple-element.148), channel_id=1, source_target_pairs={{1,0},{2,1},{3,2},{4,3},{5,4},{6,5},{7,6},{9,8},{10,9},{11,10},{12... | collective-permute-start | bytes 14408 | tf_op jit(solution)/shard_map/ppermute | solution.py:23
  155.3 11.4 %collective-permute-start.15 = (f32[5,10,3,8]{3,2,1,0:T(4,128)S(1)}, f32[5,10,3,8]{3,2,1,0:T(4,128)S(1)}, u32[]{:S(2)}, u32[]{:S(2)}) collective-permute-start(f32[5,10,3,8]{3,2,1,0:T(4,128)S(1)} %get-tuple-element.147), channel_id=1, source_target_pairs={{0,1},{1,2},{2,3},{3,4},{4,5},{5,6},{6,7},{8,9},{9,10},{10,11},{11... | collective-permute-start | bytes 14408 | tf_op jit(solution)/shard_map/ppermute | solution.py:21
  180.0 24.7 %collective-permute-start.37 = (bf16[64,1,8,8]{0,3,2,1:T(8,128)(2,1)S(1)}, bf16[64,1,8,8]{0,3,2,1:T(8,128)(2,1)S(1)}, u32[]{:S(2)}, u32[]{:S(2)}) collective-permute-start(bf16[64,1,8,8]{0,3,2,1:T(8,128)(2,1)S(1)} %get-tuple-element.283), channel_id=1, source_target_pairs={{8,0},{16,8},{24,16},{9,1},{17,9},{25,17},{10,2},{18,10},{26,18},{... | collective-permute-start | bytes 24584 | tf_op jit(solution)/shard_map/ppermute | solution.py:23
  181.3 23.4 %collective-permute-start.36 = (bf16[64,1,8,8]{0,3,2,1:T(8,128)(2,1)S(1)}, bf16[64,1,8,8]{0,3,2,1:T(8,128)(2,1)S(1)}, u32[]{:S(2)}, u32[]{:S(2)}) collective-permute-start(bf16[64,1,8,8]{0,3,2,1:T(8,128)(2,1)S(1)} %get-tuple-element.282), channel_id=1, source_target_pairs={{0,8},{8,16},{16,24},{1,9},{9,17},{17,25},{2,10},{10,18},{18,26},{... | collective-permute-start | bytes 24584 | tf_op jit(solution)/shard_map/ppermute | solution.py:21
  205.4 7.6 %collective-permute-start.39 = (bf16[64,6,1,8]{0,3,2,1:T(8,128)(2,1)S(1)}, bf16[64,6,1,8]{0,3,2,1:T(8,128)(2,1)S(1)}, u32[]{:S(2)}, u32[]{:S(2)}) collective-permute-start(bf16[64,6,1,8]{0,3,2,1:T(8,128)(2,1)S(1)} %get-tuple-element.230), channel_id=1, source_target_pairs={{1,0},{2,1},{3,2},{4,3},{5,4},{6,5},{7,6},{9,8},{10,9},{11,10},{12... | collective-permute-start | bytes 18440 | tf_op jit(solution)/shard_map/ppermute | solution.py:23
  214.1 17.3 %collective-permute-start.45 = (bf16[64,1,8,8]{0,3,2,1:T(8,128)(2,1)S(1)}, bf16[64,1,8,8]{0,3,2,1:T(8,128)(2,1)S(1)}, u32[]{:S(2)}, u32[]{:S(2)}) collective-permute-start(bf16[64,1,8,8]{0,3,2,1:T(8,128)(2,1)S(1)} %get-tuple-element.281), channel_id=1, source_target_pairs={{8,0},{16,8},{24,16},{9,1},{17,9},{25,17},{10,2},{18,10},{26,18},{... | collective-permute-start | bytes 24584 | tf_op jit(solution)/shard_map/ppermute | solution.py:23
  215.4 16.0 %collective-permute-start.44 = (bf16[64,1,8,8]{0,3,2,1:T(8,128)(2,1)S(1)}, bf16[64,1,8,8]{0,3,2,1:T(8,128)(2,1)S(1)}, u32[]{:S(2)}, u32[]{:S(2)}) collective-permute-start(bf16[64,1,8,8]{0,3,2,1:T(8,128)(2,1)S(1)} %get-tuple-element.280), channel_id=1, source_target_pairs={{0,8},{8,16},{16,24},{1,9},{9,17},{17,25},{2,10},{10,18},{18,26},{... | collective-permute-start | bytes 24584 | tf_op jit(solution)/shard_map/ppermute | solution.py:21
  249.0 7.7 %collective-permute-start.51 = (f32[8,10,3,8]{3,2,1,0:T(4,128)S(1)}, f32[8,10,3,8]{3,2,1,0:T(4,128)S(1)}, u32[]{:S(2)}, u32[]{:S(2)}) collective-permute-start(f32[8,10,3,8]{3,2,1,0:T(4,128)S(1)} %get-tuple-element.91), channel_id=1, source_target_pairs={{0,1},{1,2},{2,3},{3,4},{4,5},{5,6},{6,7},{8,9},{9,10},{10,11},{11... | collective-permute-start | bytes 23048 | tf_op jit(solution)/shard_map/ppermute | solution.py:21
  253.5 8.4 %collective-permute-start.50 = (f32[8,10,3,8]{3,2,1,0:T(4,128)S(1)}, f32[8,10,3,8]{3,2,1,0:T(4,128)S(1)}, u32[]{:S(2)}, u32[]{:S(2)}) collective-permute-start(f32[8,10,3,8]{3,2,1,0:T(4,128)S(1)} %get-tuple-element.90), channel_id=1, source_target_pairs={{1,0},{2,1},{3,2},{4,3},{5,4},{6,5},{7,6},{9,8},{10,9},{11,10},{12... | collective-permute-start | bytes 23048 | tf_op jit(solution)/shard_map/ppermute | solution.py:23
  263.9 19.7 %collective-permute-start.52 = (f32[8,3,8,8]{3,2,1,0:T(8,128)S(1)}, f32[8,3,8,8]{3,2,1,0:T(8,128)S(1)}, u32[]{:S(2)}, u32[]{:S(2)}) collective-permute-start(f32[8,3,8,8]{3,2,1,0:T(8,128)S(1)} %get-tuple-element.184), channel_id=1, source_target_pairs={{8,0},{16,8},{24,16},{9,1},{17,9},{25,17},{10,2},{18,10},{26,18},{... | collective-permute-start | bytes 18440 | tf_op jit(solution)/shard_map/ppermute | solution.py:23
  265.2 18.4 %collective-permute-start.53 = (f32[8,3,8,8]{3,2,1,0:T(8,128)S(1)}, f32[8,3,8,8]{3,2,1,0:T(8,128)S(1)}, u32[]{:S(2)}, u32[]{:S(2)}) collective-permute-start(f32[8,3,8,8]{3,2,1,0:T(8,128)S(1)} %get-tuple-element.183), channel_id=1, source_target_pairs={{0,8},{8,16},{16,24},{1,9},{9,17},{17,25},{2,10},{10,18},{18,26},{... | collective-permute-start | bytes 18440 | tf_op jit(solution)/shard_map/ppermute | solution.py:21
  277.1 13.1 %collective-permute-start.19 = (f32[5,10,3,8]{3,2,1,0:T(4,128)S(1)}, f32[5,10,3,8]{3,2,1,0:T(4,128)S(1)}, u32[]{:S(2)}, u32[]{:S(2)}) collective-permute-start(f32[5,10,3,8]{3,2,1,0:T(4,128)S(1)} %get-tuple-element.143), channel_id=1, source_target_pairs={{0,1},{1,2},{2,3},{3,4},{4,5},{5,6},{6,7},{8,9},{9,10},{10,11},{11... | collective-permute-start | bytes 14408 | tf_op jit(solution)/shard_map/ppermute | solution.py:21
  282.0 8.3 %collective-permute-start.18 = (f32[5,10,3,8]{3,2,1,0:T(4,128)S(1)}, f32[5,10,3,8]{3,2,1,0:T(4,128)S(1)}, u32[]{:S(2)}, u32[]{:S(2)}) collective-permute-start(f32[5,10,3,8]{3,2,1,0:T(4,128)S(1)} %get-tuple-element.142), channel_id=1, source_target_pairs={{1,0},{2,1},{3,2},{4,3},{5,4},{6,5},{7,6},{9,8},{10,9},{11,10},{12... | collective-permute-start | bytes 14408 | tf_op jit(solution)/shard_map/ppermute | solution.py:23
  283.7 7.8 %collective-permute-start.55 = (f32[8,10,3,8]{3,2,1,0:T(4,128)S(1)}, f32[8,10,3,8]{3,2,1,0:T(4,128)}, u32[]{:S(2)}, u32[]{:S(2)}) collective-permute-start(f32[8,10,3,8]{3,2,1,0:T(4,128)S(1)} %get-tuple-element.89), channel_id=1, source_target_pairs={{0,1},{1,2},{2,3},{3,4},{4,5},{5,6},{6,7},{8,9},{9,10},{10,11},{11... | collective-permute-start | bytes 23048 | tf_op jit(solution)/shard_map/ppermute | solution.py:21
  288.9 8.0 %collective-permute-start.54 = (f32[8,10,3,8]{3,2,1,0:T(4,128)S(1)}, f32[8,10,3,8]{3,2,1,0:T(4,128)}, u32[]{:S(2)}, u32[]{:S(2)}) collective-permute-start(f32[8,10,3,8]{3,2,1,0:T(4,128)S(1)} %get-tuple-element.88), channel_id=1, source_target_pairs={{1,0},{2,1},{3,2},{4,3},{5,4},{6,5},{7,6},{9,8},{10,9},{11,10},{12... | collective-permute-start | bytes 23048 | tf_op jit(solution)/shard_map/ppermute | solution.py:23
  299.9 71.6 %collective-permute-start.21 = (f32[5,3,8,8]{3,2,1,0:T(8,128)}, f32[5,3,8,8]{3,2,1,0:T(8,128)S(1)}, u32[]{:S(2)}, u32[]{:S(2)}) collective-permute-start(f32[5,3,8,8]{3,2,1,0:T(8,128)} %get-tuple-element.245), channel_id=1, source_target_pairs={{0,8},{8,16},{16,24},{1,9},{9,17},{17,25},{2,10},{10,18},{18,26},{... | collective-permute-start | bytes 11528 | tf_op jit(solution)/shard_map/ppermute | solution.py:21
  302.7 68.8 %collective-permute-start.20 = (f32[5,3,8,8]{3,2,1,0:T(8,128)}, f32[5,3,8,8]{3,2,1,0:T(8,128)S(1)}, u32[]{:S(2)}, u32[]{:S(2)}) collective-permute-start(f32[5,3,8,8]{3,2,1,0:T(8,128)} %get-tuple-element.244), channel_id=1, source_target_pairs={{8,0},{16,8},{24,16},{9,1},{17,9},{25,17},{10,2},{18,10},{26,18},{... | collective-permute-start | bytes 11528 | tf_op jit(solution)/shard_map/ppermute | solution.py:23
  304.3 13.8 %collective-permute-start.57 = (bf16[5,1,8,8]{3,2,1,0:T(8,128)(2,1)S(1)}, bf16[5,1,8,8]{3,2,1,0:T(8,128)(2,1)S(1)}, u32[]{:S(2)}, u32[]{:S(2)}) collective-permute-start(bf16[5,1,8,8]{3,2,1,0:T(8,128)(2,1)S(1)} %get-tuple-element.303), channel_id=1, source_target_pairs={{8,0},{16,8},{24,16},{9,1},{17,9},{25,17},{10,2},{18,10},{26,18},{... | collective-permute-start | bytes 1928 | tf_op jit(solution)/shard_map/ppermute | solution.py:23
  305.6 12.5 %collective-permute-start.56 = (bf16[5,1,8,8]{3,2,1,0:T(8,128)(2,1)S(1)}, bf16[5,1,8,8]{3,2,1,0:T(8,128)(2,1)S(1)}, u32[]{:S(2)}, u32[]{:S(2)}) collective-permute-start(bf16[5,1,8,8]{3,2,1,0:T(8,128)(2,1)S(1)} %get-tuple-element.302), channel_id=1, source_target_pairs={{0,8},{8,16},{16,24},{1,9},{9,17},{17,25},{2,10},{10,18},{18,26},{... | collective-permute-start | bytes 1928 | tf_op jit(solution)/shard_map/ppermute | solution.py:21
  328.1 10.7 %collective-permute-start.61 = (bf16[64,1,8,8]{0,3,2,1:T(8,128)(2,1)S(1)}, bf16[64,1,8,8]{0,3,2,1:T(8,128)(2,1)S(1)}, u32[]{:S(2)}, u32[]{:S(2)}) collective-permute-start(bf16[64,1,8,8]{0,3,2,1:T(8,128)(2,1)S(1)} %get-tuple-element.279), channel_id=1, source_target_pairs={{8,0},{16,8},{24,16},{9,1},{17,9},{25,17},{10,2},{18,10},{26,18},{... | collective-permute-start | bytes 24584 | tf_op jit(solution)/shard_map/ppermute | solution.py:23
  329.4 9.4 %collective-permute-start.60 = (bf16[64,1,8,8]{0,3,2,1:T(8,128)(2,1)S(1)}, bf16[64,1,8,8]{0,3,2,1:T(8,128)(2,1)S(1)}, u32[]{:S(2)}, u32[]{:S(2)}) collective-permute-start(bf16[64,1,8,8]{0,3,2,1:T(8,128)(2,1)S(1)} %get-tuple-element.278), channel_id=1, source_target_pairs={{0,8},{8,16},{16,24},{1,9},{9,17},{17,25},{2,10},{10,18},{18,26},{... | collective-permute-start | bytes 24584 | tf_op jit(solution)/shard_map/ppermute | solution.py:21
  369.3 74.4 %all-reduce.7.cloned.1.call-start = ((), (), s32[]{:S(2)}) async-start(), calls=%async_computation | async-start | bytes 1769472 | tf_op jit(solution)/shard_map/psum | solution.py:266
  371.4 145.9 %all-reduce.11.cloned.1.call-start = ((), (), s32[]{:S(2)}) async-start(), calls=%async_computation.2 | async-start | bytes 253952 | tf_op jit(solution)/shard_map/psum | solution.py:267
  371.6 8.1 %collective-permute-start.23 = (f32[5,10,3,8]{3,2,1,0:T(4,128)S(1)}, f32[5,10,3,8]{3,2,1,0:T(4,128)S(1)}, u32[]{:S(2)}, u32[]{:S(2)}) collective-permute-start(f32[5,10,3,8]{3,2,1,0:T(4,128)S(1)} %get-tuple-element.141), channel_id=1, source_target_pairs={{0,1},{1,2},{2,3},{3,4},{4,5},{5,6},{6,7},{8,9},{9,10},{10,11},{11... | collective-permute-start | bytes 14408 | tf_op jit(solution)/shard_map/ppermute | solution.py:21
  376.5 8.4 %collective-permute-start.22 = (f32[5,10,3,8]{3,2,1,0:T(4,128)S(1)}, f32[5,10,3,8]{3,2,1,0:T(4,128)S(1)}, u32[]{:S(2)}, u32[]{:S(2)}) collective-permute-start(f32[5,10,3,8]{3,2,1,0:T(4,128)S(1)} %get-tuple-element.140), channel_id=1, source_target_pairs={{1,0},{2,1},{3,2},{4,3},{5,4},{6,5},{7,6},{9,8},{10,9},{11,10},{12... | collective-permute-start | bytes 14408 | tf_op jit(solution)/shard_map/ppermute | solution.py:23
  405.6 191.0 %all-reduce.9.cloned.1.call-start = ((), (), s32[]{:S(2)}) async-start(), calls=%async_computation.1 | async-start | bytes 1769472 | tf_op jit(solution)/shard_map/psum | solution.py:267
  (126 other events, 371.8 us)
Sparse Core Ops, SparseCore 0:
  369.4 36.1 all-reduce.12
  408.0 35.6 all-reduce.6
  447.1 70.1 all-reduce.10
  520.6 75.9 all-reduce.8
